TPU v7x, 128 devices: a whole 4x4x4 slice. The times are simulated.
128 devices in a mesh: slot: 16 (over y, z), head: 2 (over x_lo), conv: 4 (over x_hi, core).
Axes of the slice: x: 4 (x_hi: 2, x_lo: 2; x = x_hi * 2 + x_lo), y: 4, z: 4, core: 2. Of those that a mesh axis runs over, the one named last changes fastest.
Arguments:
- queries: bfloat16 [1024, 64, 128], P(('conv', 'slot'), 'head'), may hold values from -96 to 96
- out_grad: bfloat16 [1024, 64, 128], P(('conv', 'slot'), 'head'), may hold values from -768 to 768
- row_positions: int32 [1024], P('conv'), may hold values from 0 to 8191
- slot_offsets: int32 [16384], P('slot'), may hold values from 0 to 16382, as said below
- cache: float32 [2, 16384, 4, 128], P(None, 'slot', 'head'), may hold values from -12 to 12
- first_moment: float32 [2, 16384, 4, 128], P(None, 'slot', 'head'), may hold values from -6 to 6
- second_moment: float32 [2, 16384, 4, 128], P(None, 'slot', 'head'), may hold values from 0.01 to 1000
Outputs:
- new_cache: float32 [2, 16384, 4, 128], P(None, 'slot', 'head')
- new_first_moment: float32 [2, 16384, 4, 128], P(None, 'slot', 'head')
- new_second_moment: float32 [2, 16384, 4, 128], P(None, 'slot', 'head')
- query_grad: float32 [1024, 64, 128], P(('conv', 'slot'), 'head')
Inputs may be any that keep to these rules, and one draw needn't show every extreme that they name: `slot_offsets`: never falls from one slot to the next; its first two entries are 0.
All inputs are finite; a program needn't handle non-finite values.
Results may differ from a plain program's by a relative error of at most 0.012.
The roundings to bfloat16 on the way count: a program that leaves them out, or rounds other values in their place, can miss the bound.
Values may be sent and summed in bfloat16 or wider, within the bound.
A program may use at most 128 MiB of HBM per device.

v0:
```python
import math

import jax
import jax.numpy as jnp
from jax import lax
from jax.sharding import PartitionSpec as P

STEP = 20


learn_rate = 0.01
beta_one = 0.9
beta_two = 0.95
adam_eps = 1e-08
masked_score = -1e30


def merged(x, axis, combine):
    everything = jax.tree.map(lambda part: lax.all_gather(part, axis), x)
    leading = jax.tree.map(lambda part: part[0], everything)

    def lap(k, so_far):
        return combine(so_far, jax.tree.map(lambda part: part[k], everything))

    return lax.fori_loop(1, lax.axis_size(axis), lap, leading)


def merge_pairs(earlier, later):
    largest = jnp.maximum(earlier[0], later[0])
    return (
        largest,
        earlier[1] * jnp.exp(earlier[0] - largest) + later[1] * jnp.exp(later[0] - largest),
    )


def local(queries, out_grad, row_positions, slot_offsets, cache, first_moment, second_moment):
    query_all, grad_all = (
        lax.all_gather(queries, "slot", axis=0, tiled=True),
        lax.all_gather(out_grad, "slot", axis=0, tiled=True),
    )
    total_rows, head_count, head_width = query_all.shape
    kv_count = cache.shape[2]
    group_heads = head_count // kv_count
    score_scale = 1.0 / math.sqrt(head_width)
    block_rows = min(64, total_rows)
    block_count = total_rows // block_rows
    key_half = cache[0].astype(jnp.bfloat16)
    value_half = cache[1].astype(jnp.bfloat16)
    query_blocks = query_all.reshape(block_count, block_rows, kv_count, group_heads, head_width)
    grad_blocks = grad_all.reshape(block_count, block_rows, kv_count, group_heads, head_width)
    visible_all = (slot_offsets[None, :] <= row_positions[:, None]).reshape(
        block_count, block_rows, -1
    )

    def masked_scores(query_block, visible):
        raw_score = (
            jnp.einsum("rkgd,skd->rkgs", query_block, key_half, preferred_element_type=jnp.float32)
            * score_scale
        )
        return jnp.where(visible[:, None, None, :], raw_score, masked_score)

    def weights_from(scores, visible, offset):
        return jnp.where(visible[:, None, None, :], jnp.exp(scores - offset[..., None]), 0.0)

    def gradient_products(grad_block):
        return jnp.einsum(
            "rkgd,skd->rkgs", grad_block, value_half, preferred_element_type=jnp.float32
        )

    def max_pass(inputs):
        query_block, visible = inputs
        scores = masked_scores(query_block, visible)
        largest = jnp.max(scores, axis=-1)
        return (largest, jnp.sum(weights_from(scores, visible, largest), axis=-1))

    largest, denominator = lax.map(max_pass, (query_blocks, visible_all))
    largest, denominator = merged((largest, denominator), "slot", merge_pairs)
    log_total = largest + jnp.log(denominator)

    def product_pass(inputs):
        query_block, grad_block, visible, block_total = inputs
        probability = weights_from(masked_scores(query_block, visible), visible, block_total)
        return jnp.sum(probability * gradient_products(grad_block), axis=-1)

    partial_sum = lax.map(product_pass, (query_blocks, grad_blocks, visible_all, log_total))
    row_sum = lax.psum(partial_sum, "slot")

    def last_pass(running, inputs):
        key_grad, value_grad = running
        query_block, grad_block, visible, block_total, block_sum = inputs
        probability = weights_from(masked_scores(query_block, visible), visible, block_total)
        prob_grad = gradient_products(grad_block)
        score_grad = (probability * (prob_grad - block_sum[..., None])).astype(jnp.bfloat16)
        prob_half = probability.astype(jnp.bfloat16)
        value_grad = value_grad + jnp.einsum(
            "rkgs,rkgd->skd", prob_half, grad_block, preferred_element_type=jnp.float32
        )
        key_grad = (
            key_grad
            + jnp.einsum(
                "rkgs,rkgd->skd", score_grad, query_block, preferred_element_type=jnp.float32
            )
            * score_scale
        )
        query_part = (
            jnp.einsum("rkgs,skd->rkgd", score_grad, key_half, preferred_element_type=jnp.float32)
            * score_scale
        )
        return ((key_grad, value_grad), query_part)

    empty_grad = jnp.zeros(key_half.shape, jnp.float32)
    (key_grad, value_grad), query_parts = lax.scan(
        last_pass,
        (empty_grad, empty_grad),
        (query_blocks, grad_blocks, visible_all, log_total, row_sum),
    )
    query_terms = query_parts.reshape(total_rows, head_count, head_width)
    summed = lax.psum(query_terms, "slot")
    own_rows = queries.shape[0]
    query_grad = lax.dynamic_slice_in_dim(summed, lax.axis_index("slot") * own_rows, own_rows, 0)
    key_total, value_total = lax.psum((key_grad, value_grad), "conv")
    slot_grad = jnp.stack([key_total, value_total])
    new_first = beta_one * first_moment + (1.0 - beta_one) * slot_grad
    new_second = beta_two * second_moment + (1.0 - beta_two) * slot_grad * slot_grad
    first_fix = 1.0 - beta_one**STEP
    second_fix = 1.0 - beta_two**STEP
    new_cache = cache - learn_rate * (new_first / first_fix) / (
        jnp.sqrt(new_second / second_fix) + adam_eps
    )
    return (new_cache, new_first, new_second, query_grad)


def solution(mesh):
    in_specs = (
        P(("conv", "slot"), "head", None),
        P(("conv", "slot"), "head", None),
        P("conv"),
        P("slot"),
        P(None, "slot", "head", None),
        P(None, "slot", "head", None),
        P(None, "slot", "head", None),
    )
    out_specs = (
        P(None, "slot", "head", None),
        P(None, "slot", "head", None),
        P(None, "slot", "head", None),
        P(("conv", "slot"), "head", None),
    )
    return jax.shard_map(local, mesh=mesh, in_specs=in_specs, out_specs=out_specs, check_vma=False)
```

profile of v0, /device:TPU:1, one launch (start us, length us, event | category | flops | bytes accessed | tf_op | source)
XLA Modules:
  0.0 525.3 jit_solution(10511550598650439508)
XLA Ops:
  9.5 1.8 copy.70
  13.1 43.8 %all-gather.5.cloned.1.call-done = bf16[256,32,128]{2,1,0:T(8,128)(2,1)} async-done(((bf16[16,32,128]{2,1,0:T(8,128)(2,1)}), bf16[256,32,128]{2,1,0:T(8,128)(2,1)}) %all-gather.5.cloned.1.call-update) | async-done | bytes 2097168 | tf_op jit(solution)/shard_map/all_gather | solution.py:38
  56.9 3.3 copy.50
  60.1 43.2 %all-gather.7.cloned.1.call-done = bf16[256,32,128]{2,1,0:T(8,128)(2,1)} async-done(((bf16[16,32,128]{2,1,0:T(8,128)(2,1)}), bf16[256,32,128]{2,1,0:T(8,128)(2,1)}) %all-gather.7.cloned.1.call-update) | async-done | bytes 2097168 | tf_op jit(solution)/shard_map/all_gather | solution.py:39
  103.3 3.3 copy.51
  106.6 23.2 %while.54 = (s32[]{:T(128)}, f32[4,64,2,16]{1,3,2,0:T(8,128)S(1)}, f32[4,64,2,16]{1,3,2,0:T(8,128)S(1)}, pred[4,64,1024]{2,1,0:T(8,128)(4,1)S(1)}, bf16[4,64,2,1...) while((s32[]{:T(128)}, f32[4,64,2,16]{1,3,2,0:T(8,128)S(1)}, ...), condition=%wide.region_3.4_spmd, body=%wide.region_0.3_spmd.sunk | while | flops 553644032 | bytes 18210912 | solution.py:76
  106.6 2.8 bitcast_reduce_fusion.2
  109.4 2.8 fusion.87
  112.4 2.8 bitcast_reduce_fusion.2
  115.2 2.8 fusion.87
  118.2 2.8 bitcast_reduce_fusion.2
  121.0 2.8 fusion.87
  124.0 2.8 bitcast_reduce_fusion.2
  126.8 2.8 fusion.87
  129.8 19.1 %all-gather.1 = f32[64,64,2,16]{1,3,2,0:T(8,128)S(1)} all-gather(f32[4,64,2,16]{1,3,2,0:T(8,128)S(1)} %get-tuple-element.272), channel_id=3, replica_groups=mesh['slot'=16,'head'=2,'conv'=4] {'slot'}, dimensions={0}, use_global_device_ids=true | all-gather | bytes 557056 | tf_op jit(solution)/shard_map/all_gather | solution.py:19
  148.9 17.4 %all-gather = f32[64,64,2,16]{1,3,2,0:T(8,128)S(1)} all-gather(f32[4,64,2,16]{1,3,2,0:T(8,128)S(1)} %get-tuple-element.271), channel_id=2, replica_groups=mesh['slot'=16,'head'=2,'conv'=4] {'slot'}, dimensions={0}, use_global_device_ids=true | all-gather | bytes 557056 | tf_op jit(solution)/shard_map/all_gather | solution.py:19
  167.2 13.9 %while.55 = (s32[]{:T(128)}, f32[4,64,2,16]{1,3,2,0:T(8,128)S(1)}, f32[4,64,2,16]{1,3,2,0:T(8,128)S(1)}, f32[16,4,64,2,16]{2,4,3,1,0:T(8,128)}, f32[16,4,64,2,16...) while((s32[]{:T(128)}, f32[4,64,2,16]{1,3,2,0:T(8,128)S(1)}, f32[4,64,2,16]{1,3,2,0:T(8,128)S(1)}, ...), condition=%wide.region_5.6_spmd, body=%wide.region_4.5_spmd.sunk | while | flops 49157 | bytes 196731 | solution.py:25
  181.5 31.2 %while.56 = (s32[]{:T(128)}, f32[4,64,2,16]{3,1,2,0:T(8,128)}, pred[4,64,1024]{2,1,0:T(8,128)(4,1)S(1)}, bf16[4,64,2,16,128]{4,3,1,2,0:T(8,128)(2,1)}, bf16[1024...) while((s32[]{:T(128)}, f32[4,64,2,16]{3,1,2,0:T(8,128)}, ...), condition=%wide.region_8.9_spmd, body=%wide.region_6.8_spmd.sunk | while | flops 1086322688 | bytes 21397652 | solution.py:85
  181.5 2.4 fusion.93
  183.9 4.7 fusion.94
  189.4 2.4 fusion.93
  191.7 4.7 fusion.94
  197.1 2.4 fusion.93
  199.5 4.7 fusion.94
  204.9 2.4 fusion.93
  207.3 4.7 fusion.94
  212.7 61.1 %psum.28 = f32[4,64,2,16]{3,1,2,0:T(8,128)S(1)} all-reduce(f32[4,64,2,16]{3,1,2,0:T(8,128)} %get-tuple-element.275), channel_id=1, replica_groups=mesh['slot'=16,'head'=2,'conv'=4] {'slot'}, use_global_device_ids=true, to_apply=%region_9.10 | all-reduce | flops 8192 | bytes 65536 | tf_op jit(solution)/shard_map/psum | solution.py:86
  273.8 52.7 %while.57 = (s32[]{:T(128)}, f32[1024,2,128]{0,2,1:T(8,128)S(1)}, f32[1024,2,128]{0,2,1:T(8,128)S(1)}, f32[4,64,2,16,128]{4,3,2,1,0:T(8,128)}, bf16[4,64,2,16,12...) while((s32[]{:T(128)}, f32[1024,2,128]{0,2,1:T(8,128)S(1)}, ...), condition=%wide.region_11.12_spmd.clone, body=%wide.region_10.11_spmd.clone.sunk | while | flops 2711093248 | bytes 59867360 | solution.py:112
  273.9 2.4 fusion.105
  276.4 2.7 fusion.108
  279.1 3.5 fusion.106
  282.5 2.1 fusion.107
  287.1 2.4 fusion.105
  289.6 2.7 fusion.108
  292.2 3.5 fusion.106
  295.7 2.1 fusion.107
  300.3 2.4 fusion.105
  302.7 2.7 fusion.108
  305.4 3.5 fusion.106
  308.9 2.1 fusion.107
  313.4 2.4 fusion.105
  315.9 2.7 fusion.108
  318.6 3.5 fusion.106
  322.1 2.1 fusion.107
  329.7 81.8 %all-reduce.6.cloned.1.call-done = (f32[1,1024,2,128]{3,2,1,0:T(2,128)}, f32[1,1024,2,128]{3,2,1,0:T(2,128)}) async-done(((f32[1,1024,2,128]{3,2,1,0:T(2,128)}, f32[1,1024,2,128]{3,2,1,0:T(2,128)}), (f32[1,1024,2,128]{3,2,1,0:T(2,128)}, f32[1,1024,2,128]{3,2,1,0:T(2,128)})) %all-reduce.6.cloned.1.call-update) | async-done | bytes 2097168 | tf_op jit(solution)/shard_map/psum | solution.py:121
  414.5 8.0 %divide_subtract_fusion = (f32[2,1024,2,128]{3,2,1,0:T(2,128)}, f32[2,1024,2,128]{3,2,1,0:T(2,128)}, f32[2,1024,2,128]{3,2,1,0:T(2,128)}) fusion(f32[2,1024,2,128]{3,2,1,0:T(2,128)S(1)} %copy-done, f32[2,1024,2,128]{3,2,1,0:T(2,128)S(1)} %constant_dynamic-update-slice_fusion.2, f32[2,1024,2,128]{3,2,1,0:T(2,128)S(1)} %copy-done.1, ...), kind=kLoop, calls=%fused_computation.80 | loop fusion | flops 6291456 | bytes 14680064 | tf_op jit(solution)/shard_map/sub | solution.py:127
  422.5 94.6 %all-reduce.4.cloned.1.call-done = f32[256,32,128]{2,1,0:T(8,128)} async-done(((f32[256,32,128]{2,1,0:T(8,128)}), f32[256,32,128]{2,1,0:T(8,128)}) %all-reduce.4.cloned.1.call-update) | async-done | bytes 4194320 | tf_op jit(solution)/shard_map/psum | solution.py:118
  517.1 1.7 constant_dynamic-slice_fusion
  (119 shorter events, 38.0 us)
Async XLA Ops:
  7.2 49.7 %all-gather.5.cloned.1.call-start = ((), (), s32[]{:S(2)}) async-start(), calls=%async_computation | async-start | bytes 2228224 | tf_op jit(solution)/shard_map/all_gather | solution.py:38
  7.9 95.4 %all-gather.7.cloned.1.call-start = ((), (), s32[]{:S(2)}) async-start(), calls=%async_computation.1 | async-start | bytes 2228224 | tf_op jit(solution)/shard_map/all_gather | solution.py:39
  8.6 402.9 %all-reduce.6.cloned.1.call-start = ((), (), s32[]{:S(2)}) async-start(), calls=%async_computation.3 | async-start | bytes 4194304 | tf_op jit(solution)/shard_map/psum | solution.py:121
  166.2 1.0 copy-start.4
  181.4 92.4 %copy-start.5 = (f32[1024,2,128]{0,2,1:T(8,128)S(1)}, f32[1024,2,128]{0,2,1:T(8,128)}, u32[]{:S(2)}) copy-start(f32[1024,2,128]{0,2,1:T(8,128)} %custom-call.1) | copy-start | bytes 3145732
  181.5 2.4 copy-start.6
  189.3 2.4 copy-start.6
  197.1 2.4 copy-start.6
  204.9 2.4 copy-start.6
  273.9 2.5 copy-start.3
  276.4 2.7 copy-start.7
  287.1 2.5 copy-start.3
  289.5 2.7 copy-start.7
  300.3 2.5 copy-start.3
  302.7 2.7 copy-start.7
  313.4 2.5 copy-start.3
  315.9 2.7 copy-start.7
  329.2 187.9 %all-reduce.4.cloned.1.call-start = ((), (), s32[]{:S(2)}) async-start(), calls=%async_computation.2 | async-start | bytes 8388608 | tf_op jit(solution)/shard_map/psum | solution.py:118
  329.2 85.2 %copy-start = (f32[2,1024,2,128]{3,2,1,0:T(2,128)S(1)}, f32[2,1024,2,128]{3,2,1,0:T(2,128)}, u32[]{:S(2)}) copy-start(f32[2,1024,2,128]{3,2,1,0:T(2,128)} %param.19) | copy-start | bytes 6291460
  411.5 3.0 copy-start.1
  411.5 3.0 copy-start.2
Sparse Core Ops, SparseCore 0:
  10.1 46.6 all-gather.4
  59.0 44.2 all-gather.6
  329.3 82.1 all-reduce.5
  414.7 102.2 all-reduce.3
where the time goes:
time: 527 us; the launch traced here: 525 us
  waiting for transfers between devices  265 us (50%)
  blocking collectives  97.6 us (19%)
  matrix products  87.2 us (17%)
  other arithmetic  33.9 us (6%)
  local copies, waits for them, and re-layouts  26.4 us (5%)
  between operations  13.9 us (3%)
    psum x1, waiting for transfers between devices, local(): summed = lax.psum(query_terms, 'slot')  94.6 us
    psum x1, waiting for transfers between devices, local(): key_total, value_total = lax.psum((key_grad, value_grad), 'conv')  81.8 us
    psum x1, blocking collectives, local(): row_sum = lax.psum(partial_sum, 'slot')  61.1 us
    all_gather x1, waiting for transfers between devices, local(): lax.all_gather(queries, 'slot', axis=0, tiled=True)  43.8 us
    all_gather x1, waiting for transfers between devices, local(): lax.all_gather(out_grad, 'slot', axis=0, tiled=True)  43.2 us
    all_gather x2, blocking collectives, merged(): everything = jax.tree.map(lambda part: lax.all_gather(part, axis), x)  36.5 us
    dot_general x8, matrix products, gradient_products(): jnp.einsum('rkgd,skd->rkgs', grad_block, value_half, preferred_element_ty...  32.8 us
    dot_general x12, matrix products, masked_scores(): jnp.einsum('rkgd,skd->rkgs', query_block, key_half, preferred_element_typ...  30.3 us
  transfers between devices with their start and end apart: 4, of which 4 were waited for; matrix products, arithmetic and copies ran while one was open for 4% of the time, Pallas kernels for 0%

commit v1 on v0

v1 whole, which is shorter than its diff:
```python
import functools
import math

import jax
import jax.numpy as jnp
from jax import lax
from jax.experimental import pallas as pl
from jax.experimental.pallas import tpu as pltpu
from jax.sharding import PartitionSpec as P

STEP = 20

SIDE = 4
STATS_CHUNK = 256
GRADS_CHUNK = 512
REDUCE_LAG = 2

learn_rate = 0.01
beta_one = 0.9
beta_two = 0.95
adam_eps = 1e-08
masked_score = -1e30

MESH = pl.DeviceIdType.MESH
BF16 = jnp.bfloat16
F32 = jnp.float32


def nt(a, b):
    return lax.dot_general(a, b, (((1,), (1,)), ((), ())), preferred_element_type=F32)


def nn(a, b):
    return lax.dot_general(a, b, (((1,), (0,)), ((), ())), preferred_element_type=F32)


def lanes(column, width):
    return jnp.concatenate([column] * (width // column.shape[1]), axis=1)


def stats_pass(q, g, key_ref, value_ref, offset_ref, position, score_scale, chunk):
    width = q.shape[0]
    largest = jnp.full((8, width), masked_score, F32)
    total = jnp.zeros((8, width), F32)
    product = jnp.zeros((8, width), F32)
    for at in range(0, key_ref.shape[0], chunk):
        score = nt(key_ref[at : at + chunk], q)
        prob_grad = nt(value_ref[at : at + chunk], g)
        visible = lanes(offset_ref[at : at + chunk], width) <= position
        score = jnp.where(visible, score * score_scale, masked_score).reshape(chunk // 8, 8, width)
        now = jnp.maximum(largest, score.max(0))
        weight = jnp.exp2(score - now[None])
        fade = jnp.exp2(largest - now)
        total = total * fade + weight.sum(0)
        product = product * fade + (weight * prob_grad.reshape(chunk // 8, 8, width)).sum(0)
        largest = now
    top = largest.max(0, keepdims=True)
    fade = jnp.exp2(largest - top)
    return top, (total * fade).sum(0, keepdims=True), (product * fade).sum(0, keepdims=True)


def grad_pass(q, g, key_ref, value_ref, key_t_ref, offset_ref, position, log_total, row_sum, key_grad, value_grad, score_scale, chunk):
    width = q.shape[0]
    query_grad = jnp.zeros((q.shape[1], width), F32)
    for at in range(0, key_ref.shape[0], chunk):
        part = slice(at, at + chunk)
        score = nt(key_ref[part], q)
        prob_grad = nt(value_ref[part], g)
        visible = lanes(offset_ref[part], width) <= position
        probability = jnp.where(visible, jnp.exp2(score * score_scale - log_total), 0.0)
        score_grad = (probability * (prob_grad - row_sum)).astype(BF16)
        value_grad[part] += nn(probability.astype(BF16), g)
        key_grad[part] += nn(score_grad, q)
        query_grad = query_grad + nn(key_t_ref[:, part], score_grad)
    return query_grad


NEAR_FIRST = ((0, 0), (0, 1), (0, 3), (1, 0), (3, 0), (1, 1), (1, 3), (3, 1), (3, 3), (0, 2), (2, 0), (1, 2), (3, 2), (2, 1), (2, 3), (2, 2))
FAR_FIRST = ((2, 2), (2, 1), (1, 2), (2, 3), (3, 2), (1, 1), (1, 3), (3, 1), (3, 3), (2, 0), (0, 2), (1, 0), (3, 0), (0, 1), (0, 3), (0, 0))


def looked_up(table, at):
    found = jnp.int32(table[0])
    for i in range(1, len(table)):
        found = found + (table[i] - table[i - 1]) * jnp.where(at >= i, 1, 0)
    return found


def whole_kernel(
    scale,
    query_in,
    grad_in,
    position_ref,
    offset_ref,
    cache_in,
    slot_grad_out,
    query_grad_out,
    q_all,
    g_all,
    stage,
    key_ref,
    value_ref,
    key_t_ref,
    key_grad,
    value_grad,
    own_stats,
    stats_in,
    known,
    terms,
    far_one,
    near_one,
    far_two,
    near_two,
    core_out,
    core_in,
    chip_out,
    chip_in,
    total_out,
    total_in,
    load_sem,
    gather_send,
    gather_recv,
    stats_send,
    stats_recv,
    known_send,
    known_recv,
    reduce_send,
    far_one_recv,
    near_one_recv,
    far_two_recv,
    near_two_recv,
    conv_send,
    conv_recv,
):
    n_slot = SIDE * SIDE
    kv_count, slots, head_width = key_ref.shape
    group = q_all.shape[3]
    own_rows = q_all.shape[2]
    width = own_rows * group
    half_rows = own_rows // 2
    scale2 = scale * math.log2(math.e)
    me = lax.axis_index("slot")
    my_y, my_z = me // SIDE, me % SIDE
    conv = lax.axis_index("conv")
    core = conv % 2
    sibling = conv + 1 - 2 * core
    partner = (conv + 2) % 4

    def slot_at(y, z):
        return ((y + SIDE) % SIDE) * SIDE + (z + SIDE) % SIDE

    barrier = pltpu.get_barrier_semaphore()

    def greet(i, _):
        pl.semaphore_signal(barrier, inc=1, device_id={"slot": (me + i) % n_slot}, device_id_type=MESH)
        return 0

    lax.fori_loop(1, n_slot, greet, 0)
    pl.semaphore_signal(barrier, inc=1, device_id={"conv": sibling}, device_id_type=MESH)
    pl.semaphore_signal(barrier, inc=1, device_id={"conv": partner}, device_id_type=MESH)

    loads = []
    for i, (source, target) in enumerate(((query_in, q_all), (grad_in, g_all))):
        for k in range(kv_count):
            loads.append(pltpu.make_async_copy(source.at[:, k * group : (k + 1) * group, :], target.at[k, me], load_sem.at[i, k]))
    cache_load = pltpu.make_async_copy(cache_in, stage, load_sem.at[2, 0])
    for load in loads:
        load.start()
    cache_load.start()
    for load in loads:
        load.wait()
    pl.semaphore_wait(barrier, n_slot + 1)

    def gather_copy(tensor, k, block, piece, device, sem_piece):
        buffer = (q_all, g_all)[tensor]
        view = buffer.at[k, block] if piece is None else buffer.at[k, block, pl.ds(piece * half_rows, half_rows)]
        return pltpu.make_async_remote_copy(
            src_ref=view,
            dst_ref=view,
            send_sem=gather_send.at[tensor, k],
            recv_sem=gather_recv.at[tensor, k, block, sem_piece],
            device_id={"slot": device},
            device_id_type=MESH,
        )

    def ring(tensor, first, step):
        along_y = (tensor == 0) == first
        return slot_at(my_y + step, my_z) if along_y else slot_at(my_y, my_z + step)

    def gather_own(k):
        for tensor in (0, 1):
            for first in (True, False):
                for step in (1, -1):
                    gather_copy(tensor, k, me, None, ring(tensor, first, step), 0).start()

    def gather_event(k, dy, dz):
        block = slot_at(my_y + dy, my_z + dz)
        for tensor in (0, 1):
            da, db = (dy, dz) if tensor == 0 else (dz, dy)
            halves = (db == 2) | ((db == 0) & (da == 2))
            own = (da == 0) & (db == 0)

            @pl.when(halves)
            def _():
                for piece in (0, 1):
                    gather_copy(tensor, k, block, piece, me, piece).wait_recv()

            @pl.when(jnp.logical_not(halves | own))
            def _():
                gather_copy(tensor, k, block, None, me, 0).wait_recv()

            @pl.when((db == 0) & (da == 3))
            def _():
                gather_copy(tensor, k, block, 0, ring(tensor, True, 1), 0).start()

            @pl.when((db == 0) & (da == 1))
            def _():
                gather_copy(tensor, k, block, 1, ring(tensor, True, -1), 1).start()

            @pl.when((db == 0) & (da != 0))
            def _():
                gather_copy(tensor, k, block, None, ring(tensor, False, 1), 0).start()
                gather_copy(tensor, k, block, None, ring(tensor, False, -1), 0).start()

            @pl.when(db == 3)
            def _():
                gather_copy(tensor, k, block, 0, ring(tensor, False, 1), 0).start()

            @pl.when(db == 1)
            def _():
                gather_copy(tensor, k, block, 1, ring(tensor, False, -1), 1).start()

    gather_own(0)

    cache_load.wait()
    for k in range(kv_count):
        key = stage[0, pl.ds(k, slots, stride=kv_count), :]
        key_ref[k] = key.astype(BF16)
        key_t_ref[k] = key.T.astype(BF16)
        value_ref[k] = stage[1, pl.ds(k, slots, stride=kv_count), :].astype(BF16)
    key_grad[...] = jnp.zeros_like(key_grad)
    value_grad[...] = jnp.zeros_like(value_grad)

    def all_slots(k, source, target, send_sem, recv_sem, own_source):
        def send(i, _):
            other = (me + i) % n_slot
            pltpu.make_async_remote_copy(
                src_ref=source.at[k, me if own_source else other],
                dst_ref=target.at[k, me],
                send_sem=send_sem.at[k],
                recv_sem=recv_sem.at[k],
                device_id={"slot": other},
                device_id_type=MESH,
            ).start()
            return 0

        lax.fori_loop(1, n_slot, send, 0)

    def wait_all(k, ref, sem):
        view = ref.at[k, pl.ds(0, n_slot - 1)]
        pltpu.make_async_copy(view, view, sem.at[k]).wait()

    def stats_out(k):
        all_slots(k, own_stats, stats_in, stats_send, stats_recv, False)

    def stats_combine(k):
        wait_all(k, stats_in, stats_recv)
        stats_in[k, me] = own_stats[k, me]
        every = stats_in[k]
        top = every[:, 0:2].max(0)
        fade = jnp.exp2(every[:, 0:2] - top[None])
        total = (every[:, 2:4] * fade).sum(0)
        row_sum = (every[:, 4:6] * fade).sum(0) / total
        known[k, me, 0:2] = top + jnp.log2(total)
        known[k, me, 2:4] = row_sum
        all_slots(k, known, known, known_send, known_recv, True)

    def rows_of(ref, k, block):
        return ref[k, block].reshape(width, head_width)

    def stats_step(t, _):
        k, at = t // n_slot, t % n_slot
        dy, dz = looked_up([d[0] for d in NEAR_FIRST], at), looked_up([d[1] for d in NEAR_FIRST], at)
        block = slot_at(my_y + dy, my_z + dz)

        @pl.when(t == n_slot)
        def _():
            stats_out(0)

        @pl.when(t == n_slot // 2)
        def _():
            gather_own(1)

        @pl.when(t == n_slot + 6)
        def _():
            stats_combine(0)

        gather_event(k, dy, dz)
        stats = stats_pass(
            rows_of(q_all, k, block),
            rows_of(g_all, k, block),
            key_ref.at[k],
            value_ref.at[k],
            offset_ref,
            position_ref[block],
            scale2,
            STATS_CHUNK,
        )
        for i, stat in enumerate(stats):
            for j in range(width // 128):
                row = i * (width // 128) + j
                own_stats[k, block, row : row + 1] = stat[:, j * 128 : (j + 1) * 128]
        return 0

    lax.fori_loop(0, kv_count * n_slot, stats_step, 0)
    stats_out(1)

    def reduce_copy(color, k, source, target, recv_sem, device):
        return pltpu.make_async_remote_copy(
            src_ref=source,
            dst_ref=target,
            send_sem=reduce_send.at[k, color],
            recv_sem=recv_sem,
            device_id={"slot": device},
            device_id_type=MESH,
        )

    quarter = head_width // 4

    def reduce_event(k, dy, dz):
        block = slot_at(my_y + dy, my_z + dz)
        for color in (0, 1):
            da, db = (dy, dz) if color == 0 else (dz, dy)
            a_at = ((my_y if color == 0 else my_z) + da) % SIDE
            mine = terms.at[k, color, block]

            def arrived(target, sem):
                pltpu.make_async_copy(target, target, sem).wait()
                return target[...].astype(F32)

            def add(rows, value):
                mine[rows] = (mine[rows].astype(F32) + value).astype(BF16)

            def pieces(target, sems, first, index):
                for side, step in ((0, 1), (1, -1)):
                    place = (k, color, side) + index
                    rows = mine.at[pl.ds(side * quarter, quarter)]
                    reduce_copy(color, k, rows, target.at[place], sems.at[place], ring(color, first, step)).start()

            def onward(target, sems, first, index, side):
                place = (k, color, side) + index
                reduce_copy(color, k, mine, target.at[place], sems.at[place], ring(color, first, 1 - 2 * side)).start()

            @pl.when(db == 2)
            def _():
                pieces(far_one, far_one_recv, False, (a_at,))

            for side, step in ((0, 1), (1, 3)):

                @pl.when(db == step)
                def _():
                    place = (k, color, side, a_at)
                    add(pl.ds(side * quarter, quarter), arrived(far_one.at[place], far_one_recv.at[place]))
                    onward(near_one, near_one_recv, False, (a_at,), side)

            @pl.when(db == 0)
            def _():
                total = mine[...].astype(F32)
                for side in (0, 1):
                    place = (k, color, side, a_at)
                    total = total + arrived(near_one.at[place], near_one_recv.at[place])
                mine[...] = total.astype(BF16)

                @pl.when(da == 2)
                def _():
                    pieces(far_two, far_two_recv, True, ())

                for side, step in ((0, 1), (1, 3)):

                    @pl.when(da == step)
                    def _():
                        place = (k, color, side)
                        add(pl.ds(side * quarter, quarter), arrived(far_two.at[place], far_two_recv.at[place]))
                        onward(near_two, near_two_recv, True, (), side)

    def reduce_end(k):
        sums = []
        for color in (0, 1):
            total = terms[k, color, me].astype(F32)
            for side in (0, 1):
                place = (k, color, side)
                view = near_two.at[place]
                pltpu.make_async_copy(view, view, near_two_recv.at[place]).wait()
                total = total + view[...].astype(F32)
            sums.append(total)
        rows = jnp.concatenate(sums, axis=0).T.reshape(own_rows, group, head_width)
        query_grad_out[:, k * group : (k + 1) * group, :] = rows

    half = slots // 2

    def conv_copy(source, target, place, device):
        return pltpu.make_async_remote_copy(
            src_ref=source,
            dst_ref=target,
            send_sem=conv_send.at[place],
            recv_sem=conv_recv.at[place],
            device_id={"conv": device},
            device_id_type=MESH,
        )

    def conv_one(k):
        theirs = pl.ds(pl.multiple_of((1 - core) * half, half), half)
        core_out[k, 0] = (key_grad[k, theirs, :] * scale).astype(BF16)
        core_out[k, 1] = value_grad[k, theirs, :].astype(BF16)
        conv_copy(core_out.at[k], core_in.at[k], (k, 0), sibling).start()

    def conv_two(k):
        conv_copy(core_out.at[k], core_in.at[k], (k, 0), sibling).wait_recv()
        ours = pl.ds(pl.multiple_of(core * half, half), half)
        chip_out[k, 0] = (key_grad[k, ours, :] * scale + core_in[k, 0].astype(F32)).astype(BF16)
        chip_out[k, 1] = (value_grad[k, ours, :] + core_in[k, 1].astype(F32)).astype(BF16)
        conv_copy(chip_out.at[k], chip_in.at[k], (k, 1), partner).start()

    def store_total(k, owner, value):
        for i in (0, 1):
            place = pl.ds(pl.multiple_of(owner * (half * kv_count), half * kv_count) + k, half, stride=kv_count)
            slot_grad_out[i, place, :] = value[i]

    def conv_three(k):
        conv_copy(chip_out.at[k], chip_in.at[k], (k, 1), partner).wait_recv()
        total_out[k] = (chip_out[k].astype(F32) + chip_in[k].astype(F32)).astype(BF16)
        conv_copy(total_out.at[k], total_in.at[k], (k, 2), sibling).start()
        store_total(k, core, total_out[k].astype(F32))

    def conv_end(k):
        conv_copy(total_out.at[k], total_in.at[k], (k, 2), sibling).wait_recv()
        store_total(k, 1 - core, total_in[k].astype(F32))
        for i in range(3):
            conv_copy(total_out.at[k], total_in.at[k], (k, i), sibling).wait_send()

    wait_all(0, known, known_recv)

    steps = kv_count * n_slot

    def order_at(t):
        at = t % n_slot
        return t // n_slot, looked_up([d[0] for d in FAR_FIRST], at), looked_up([d[1] for d in FAR_FIRST], at)

    def grads_step(t, _):
        @pl.when(t == 6)
        def _():
            stats_combine(1)

        @pl.when(t == n_slot)
        def _():
            wait_all(1, known, known_recv)
            conv_one(0)

        @pl.when(t == n_slot + 4)
        def _():
            conv_two(0)

        @pl.when(t == n_slot + 13)
        def _():
            conv_three(0)

        @pl.when(t >= REDUCE_LAG)
        def _():
            reduce_event(*order_at(t - REDUCE_LAG))

        @pl.when(t < steps)
        def _():
            k, dy, dz = order_at(t)
            block = slot_at(my_y + dy, my_z + dz)
            stats = known[k, block]
            both = [jnp.concatenate([stats[i : i + 1], stats[i + 1 : i + 2]], axis=1) for i in (0, 2)]
            found = grad_pass(
                rows_of(q_all, k, block),
                rows_of(g_all, k, block),
                key_ref.at[k],
                value_ref.at[k],
                key_t_ref.at[k],
                offset_ref,
                position_ref[block],
                both[0],
                both[1],
                key_grad.at[k],
                value_grad.at[k],
                scale2,
                GRADS_CHUNK,
            )
            found = (found * scale).astype(BF16)
            for color in (0, 1):
                terms[k, color, block] = found[color * head_width // 2 : (color + 1) * head_width // 2]

        @pl.when(t == steps)
        def _():
            conv_one(1)

        return 0

    lax.fori_loop(0, steps + REDUCE_LAG, grads_step, 0)
    conv_two(1)
    reduce_end(0)
    conv_end(0)
    reduce_end(1)
    conv_three(1)
    for k in range(kv_count):
        for tensor, buffer in enumerate((q_all, g_all)):
            view = buffer.at[k, pl.ds(0, n_slot - 1)]
            pltpu.make_async_copy(view, view, gather_send.at[tensor, k]).wait()
        wait_all(k, own_stats, stats_send)
        wait_all(k, known, known_send)
        for color in (0, 1):
            view = terms.at[k, color, pl.ds(0, n_slot - 1)]
            pltpu.make_async_copy(view, view, reduce_send.at[k, color]).wait()
    conv_end(1)


def local(queries, out_grad, row_positions, slot_offsets, cache, first_moment, second_moment):
    own_rows, head_count, head_width = queries.shape
    kv_count, slots = cache.shape[2], cache.shape[1]
    group = head_count // kv_count
    blocks = row_positions.shape[0] // own_rows
    width = own_rows * group
    scale = 1.0 / math.sqrt(head_width)

    offsets = jnp.broadcast_to(slot_offsets[:, None], (slots, 128))
    positions = jnp.repeat(row_positions, group).reshape(blocks, 1, width)
    flat = (2, slots * kv_count, head_width)

    vmem = pl.BlockSpec(memory_space=pltpu.VMEM)
    hbm = pl.BlockSpec(memory_space=pl.ANY)
    dma = pltpu.SemaphoreType.DMA
    rows_all = pltpu.VMEM((kv_count, blocks, own_rows, group, head_width), BF16)
    slots_half = pltpu.VMEM((kv_count, slots, head_width), BF16)
    slots_full = pltpu.VMEM((kv_count, slots, head_width), F32)
    stats = pltpu.VMEM((kv_count, blocks, 8, 128), F32)
    conv_half = pltpu.VMEM((kv_count, 2, slots // 2, head_width), BF16)
    slot_grad, query_grad = pl.pallas_call(
        functools.partial(whole_kernel, scale),
        out_shape=(jax.ShapeDtypeStruct(flat, F32), jax.ShapeDtypeStruct(queries.shape, F32)),
        in_specs=[hbm, hbm, vmem, vmem, hbm],
        out_specs=(vmem, vmem),
        scratch_shapes=[
            rows_all,
            rows_all,
            pltpu.VMEM(flat, F32),
            slots_half,
            slots_half,
            pltpu.VMEM((kv_count, head_width, slots), BF16),
            slots_full,
            slots_full,
            stats,
            stats,
            stats,
            pltpu.VMEM((kv_count, 2, blocks, head_width // 2, width), BF16),
            pltpu.VMEM((kv_count, 2, 2, SIDE, head_width // 4, width), BF16),
            pltpu.VMEM((kv_count, 2, 2, SIDE, head_width // 2, width), BF16),
            pltpu.VMEM((kv_count, 2, 2, head_width // 4, width), BF16),
            pltpu.VMEM((kv_count, 2, 2, head_width // 2, width), BF16),
        ]
        + [conv_half] * 6
        + [
            dma((3, kv_count)),
            dma((2, kv_count)),
            dma((2, kv_count, blocks, 2)),
            dma((kv_count,)),
            dma((kv_count,)),
            dma((kv_count,)),
            dma((kv_count,)),
            dma((kv_count, 2)),
            dma((kv_count, 2, 2, SIDE)),
            dma((kv_count, 2, 2, SIDE)),
            dma((kv_count, 2, 2)),
            dma((kv_count, 2, 2)),
            dma((kv_count, 3)),
            dma((kv_count, 3)),
        ],
        compiler_params=pltpu.CompilerParams(collective_id=0, has_side_effects=True, vmem_limit_bytes=48 << 20),
        name="whole",
    )(queries, out_grad, positions, offsets, cache.reshape(flat))

    first_flat, second_flat, cache_flat = (x.reshape(flat) for x in (first_moment, second_moment, cache))
    new_first = beta_one * first_flat + (1.0 - beta_one) * slot_grad
    new_second = beta_two * second_flat + (1.0 - beta_two) * slot_grad * slot_grad
    first_fix = 1.0 - beta_one**STEP
    second_fix = 1.0 - beta_two**STEP
    new_cache = cache_flat - learn_rate * (new_first / first_fix) / (jnp.sqrt(new_second / second_fix) + adam_eps)
    return tuple(x.reshape(cache.shape) for x in (new_cache, new_first, new_second)) + (query_grad,)


def solution(mesh):
    rows = P(("conv", "slot"), "head", None)
    slots = P(None, "slot", "head", None)
    return jax.shard_map(
        local,
        mesh=mesh,
        in_specs=(rows, rows, P("conv"), P("slot"), slots, slots, slots),
        out_specs=(slots, slots, slots, rows),
        check_vma=False,
    )
```

time: 527 us -> 121 us (0.23)
  waiting for transfers between devices: 265 us -> 0 us
  Pallas kernels: 0 us -> 108 us
  blocking collectives: 97.6 us -> 0 us
  matrix products: 87.2 us -> 0 us
  other arithmetic: 33.9 us -> 5.46 us
  local copies, waits for them, and re-layouts: 26.4 us -> 6.44 us
  between operations: 13.9 us -> 0.7 us
    psum x2 -> x0, waiting for transfers between devices: 176 us -> none  [the longest x1 94.6 us: local(): summed = lax.psum(query_terms, 'slot')]
    pallas_call x0 -> x1, Pallas kernels: none -> 108 us  [local(): pl.pallas_call(functools.partial(whole_kernel, scale), out_shape=(jax.Sha...]
    dot_general x32 -> x0, matrix products: 87.2 us -> none  [the longest x8 32.8 us: gradient_products(): jnp.einsum('rkgd,skd->rkgs', grad_block, value_half, preferred_element_ty...]
    all_gather x2 -> x0, waiting for transfers between devices: 86.9 us -> none  [the longest x1 43.8 us: local(): lax.all_gather(queries, 'slot', axis=0, tiled=True)]
    psum x1 -> x0, blocking collectives: 61.1 us -> none  [local(): row_sum = lax.psum(partial_sum, 'slot')]
    all_gather x2 -> x0, blocking collectives: 36.5 us -> none  [merged(): everything = jax.tree.map(lambda part: lax.all_gather(part, axis), x)]
    add x16 -> x0, other arithmetic: 13.7 us -> none  [the longest x15 13.6 us: merge_pairs(): earlier[1] * jnp.exp(earlier[0] - largest)]
    reduce_sum x4 -> x0, other arithmetic: 11.4 us -> none  [max_pass(): return (largest, jnp.sum(weights_from(scores, visible, largest), axis=-1))]
  transfers between devices with their start and end apart: 4 -> 0, of which waited for: 4 -> 0; matrix products, arithmetic and copies ran while one was open for 4% -> 0% of each run, Pallas kernels for 0% -> 0%
where the time goes in v1:
time: 121 us
  Pallas kernels  108 us (89%)
  local copies, waits for them, and re-layouts  6.44 us (5%)
  other arithmetic  5.46 us (5%)
    pallas_call x1, Pallas kernels, local(): pl.pallas_call(functools.partial(whole_kernel, scale), out_shape=(jax.Sha...  108 us
    unnamed x11, local copies, waits for them, and re-layouts  4.6 us
    sub x1, other arithmetic, local(): cache_flat - learn_rate * (new_first / first_fix) / (jnp.sqrt(new_second...  3.3 us

profile of v1, /device:TPU:1, one launch (start us, length us, event | category | flops | bytes accessed | tf_op | source)
XLA Modules:
  0.0 121.0 jit_solution(2331963618312510766)
XLA Ops:
  0.6 0.8 broadcast_in_dim.13
  1.4 0.1 broadcast_in_dim.14
  1.5 0.1 broadcast_in_dim.15.position_ref
  1.6 0.9 broadcast_in_dim.16.offset_ref
  2.5 0.0 copy-start
  2.5 1.6 %copy-done = f32[2,1024,2,128]{3,2,1,0:T(2,128)S(1)} copy-done((f32[2,1024,2,128]{3,2,1,0:T(2,128)S(1)}, f32[2,1024,2,128]{3,2,1,0:T(2,128)}, u32[]{:S(2)}) %copy-start) | copy-done | bytes 2097176
  4.1 0.0 copy-start.1
  4.1 0.9 copy-done.1
  5.0 0.0 copy-start.2
  5.0 0.9 copy-done.2
  5.9 0.0 copy-start.3
  5.9 108.4 %whole.1 = (f32[2,2048,128]{2,1,0:T(8,128)S(1)}, f32[16,32,128]{2,1,0:T(8,128)S(1)}) custom-call(bf16[16,32,128]{2,1,0:T(8,128)(2,1)S(1)} %copy-done.1, bf16[16,32,128]{2,1,0:T(8,128)(2,1)S(1)} %copy-done.2, s32[16,1,256]{2,1,0:T(1,128)S(1)} %broadcast_in_dim.15.position_ref, s32[1024,128]{1,0:T(8,128)S(1)} %broadcast_in_dim.16.offset_ref, ...), custom_call_target="tpu_custom_call" | custom-call | tf_op jit(solution)/shard_map/whole/pallas_call | solution.py:540
  114.3 0.0 copy-done.3
  114.3 0.0 copy-start.4
  114.3 1.1 broadcast_multiply_fusion.1
  115.4 0.5 copy-done.4
  115.9 1.1 broadcast_multiply_fusion
  117.0 3.3 %divide_subtract_fusion = (f32[2,2048,128]{2,1,0:T(8,128)}, f32[2,2048,128]{2,1,0:T(8,128)}, f32[2,2048,128]{2,1,0:T(8,128)}) fusion(f32[2,2048,128]{2,1,0:T(8,128)S(1)} %bitcast.7, f32[2,2048,128]{2,1,0:T(8,128)S(1)} %bitcast.8, f32[2,2048,128]{2,1,0:T(8,128)S(1)} %get-tuple-element.6, f32[2,2048,128]{2,1,0:T(8,128)S(1)} %bitcast.9), kind=kLoop, calls=%fused_computation.2 | loop fusion | flops 5242880 | bytes 14680064 | tf_op jit(solution)/shard_map/sub | solution.py:589
  120.3 0.7 copy.12
Async XLA Ops:
  2.5 1.6 %copy-start = (f32[2,1024,2,128]{3,2,1,0:T(2,128)S(1)}, f32[2,1024,2,128]{3,2,1,0:T(2,128)}, u32[]{:S(2)}) copy-start(f32[2,1024,2,128]{3,2,1,0:T(2,128)} %param.11) | copy-start | bytes 6291460
  4.1 0.9 copy-start.1
  5.0 0.9 copy-start.2
  5.9 108.4 %copy-start.3 = (f32[2,1024,2,128]{3,2,1,0:T(2,128)S(1)}, f32[2,1024,2,128]{3,2,1,0:T(2,128)}, u32[]{:S(2)}) copy-start(f32[2,1024,2,128]{3,2,1,0:T(2,128)} %param.12) | copy-start | bytes 6291460
  114.3 1.6 %copy-start.4 = (f32[2,1024,2,128]{3,2,1,0:T(2,128)S(1)}, f32[2,1024,2,128]{3,2,1,0:T(2,128)}, u32[]{:S(2)}) copy-start(f32[2,1024,2,128]{3,2,1,0:T(2,128)} %param.13) | copy-start | bytes 6291460

commit v2 on v1

v2 whole, which is shorter than its diff:
```python
import functools
import math

import jax
import jax.numpy as jnp
from jax import lax
from jax.experimental import pallas as pl
from jax.experimental.pallas import tpu as pltpu
from jax.sharding import PartitionSpec as P

STEP = 20

SIDE = 4
STATS_CHUNK = 256
GRADS_CHUNK = 256

learn_rate = 0.01
beta_one = 0.9
beta_two = 0.95
adam_eps = 1e-08
masked_score = -1e30

MESH = pl.DeviceIdType.MESH
BF16 = jnp.bfloat16
F32 = jnp.float32


def nt(a, b):
    return lax.dot_general(a, b, (((1,), (1,)), ((), ())), preferred_element_type=F32)


def nn(a, b):
    return lax.dot_general(a, b, (((1,), (0,)), ((), ())), preferred_element_type=F32)


def lanes(column, width):
    return jnp.concatenate([column] * (width // column.shape[1]), axis=1)


def stats_pass(q, g, key_ref, value_ref, offset_ref, position, score_scale, chunk):
    width = q.shape[0]
    largest = jnp.full((8, width), masked_score, F32)
    total = jnp.zeros((8, width), F32)
    product = jnp.zeros((8, width), F32)
    for at in range(0, key_ref.shape[0], chunk):
        score = nt(key_ref[at : at + chunk], q)
        prob_grad = nt(value_ref[at : at + chunk], g)
        visible = lanes(offset_ref[at : at + chunk], width) <= position
        score = jnp.where(visible, score * score_scale, masked_score).reshape(chunk // 8, 8, width)
        now = jnp.maximum(largest, score.max(0))
        weight = jnp.exp2(score - now[None])
        fade = jnp.exp2(largest - now)
        total = total * fade + weight.sum(0)
        product = product * fade + (weight * prob_grad.reshape(chunk // 8, 8, width)).sum(0)
        largest = now
    top = largest.max(0, keepdims=True)
    fade = jnp.exp2(largest - top)
    return top, (total * fade).sum(0, keepdims=True), (product * fade).sum(0, keepdims=True)


def grad_pass(q, g, key_ref, value_ref, key_t_ref, offset_ref, position, log_total, row_sum, key_grad, value_grad, score_scale, chunk):
    width = q.shape[0]
    query_grad = jnp.zeros((q.shape[1], width), F32)
    for at in range(0, key_ref.shape[0], chunk):
        part = slice(at, at + chunk)
        score = nt(key_ref[part], q)
        prob_grad = nt(value_ref[part], g)
        visible = lanes(offset_ref[part], width) <= position
        probability = jnp.where(visible, jnp.exp2(score * score_scale - log_total), 0.0)
        score_grad = (probability * (prob_grad - row_sum)).astype(BF16)
        value_grad[part] += nn(probability.astype(BF16), g)
        key_grad[part] += nn(score_grad, q)
        query_grad = query_grad + nn(key_t_ref[:, part], score_grad)
    return query_grad


NEAR_FIRST = ((0, 0), (0, 1), (0, 3), (1, 0), (3, 0), (0, 2), (2, 0), (1, 1), (1, 3), (3, 1), (3, 3), (2, 1), (2, 3), (1, 2), (3, 2), (2, 2))
FAR_FIRST = ((2, 2), (2, 1), (1, 2), (2, 3), (3, 2), (2, 0), (0, 2), (1, 1), (1, 3), (3, 1), (3, 3), (1, 0), (3, 0), (0, 1), (0, 3), (0, 0))
STEPS = (
    [(0, 0, p) for p in range(8)]
    + [(0, 1, p) for p in range(3)]
    + [(1, 0, p) for p in range(4)]
    + [(0, 1, p) for p in range(3, 8)]
    + [(1, 0, p) for p in range(4, 8)]
    + [(1, 1, p) for p in range(8)]
)
REDUCE = (
    ((0, 2, 2), (1, 2, 2), (1, 1, 2)),
    ((0, 1, 2), (1, 3, 2)),
    ((0, 3, 2), (0, 2, 1), (0, 2, 3), (1, 0, 2), (1, 2, 1), (1, 2, 3)),
    ((0, 0, 2), (0, 1, 1), (1, 1, 1)),
    ((0, 1, 3), (0, 3, 1), (0, 2, 0), (1, 1, 3), (1, 3, 1), (1, 2, 0)),
    ((0, 3, 3), (1, 3, 3), (1, 0, 1)),
    ((0, 0, 1), (0, 1, 0), (1, 0, 3), (1, 1, 0)),
    ((0, 0, 3), (0, 3, 0), (1, 3, 0)),
    (),
    ((0, 0, 0), (1, 0, 0)),
)
REDUCE_AT = ((13, 14, 15, 17, 21, 22, 23, 24, 25, 26), (25, 26, 27, 28, 29, 30, 31))


def looked_up(table, at):
    found = jnp.int32(table[0])
    for i in range(1, len(table)):
        if table[i] != table[i - 1]:
            found = found + (table[i] - table[i - 1]) * jnp.where(at >= i, 1, 0)
    return found


def whole_kernel(
    scale,
    query_in,
    grad_in,
    position_hbm,
    offset_hbm,
    cache_in,
    first_in,
    second_in,
    slot_grad_out,
    query_grad_out,
    stage,
    first_out,
    second_out,
    position_in,
    offset_in,
    position_ref,
    offset_ref,
    q_all,
    g_all,
    key_ref,
    value_ref,
    key_t_ref,
    key_grad,
    value_grad,
    own_stats,
    stats_in,
    known,
    terms,
    far_one,
    near_one,
    far_two,
    near_two,
    core_out,
    core_in,
    chip_out,
    chip_in,
    total_out,
    total_in,
    load_sem,
    gather_send,
    gather_recv,
    stats_send,
    stats_recv,
    known_send,
    known_recv,
    reduce_send,
    far_one_recv,
    near_one_recv,
    far_two_recv,
    near_two_recv,
    conv_send,
    conv_recv,
):
    n_slot = SIDE * SIDE
    kv_count, slots, head_width = key_ref.shape
    group = q_all.shape[3]
    own_rows = q_all.shape[2]
    width = own_rows * group
    scale2 = scale * math.log2(math.e)
    me = lax.axis_index("slot")
    my_y, my_z = me // SIDE, me % SIDE
    conv = lax.axis_index("conv")
    core = conv % 2
    sibling = conv + 1 - 2 * core
    partner = (conv + 2) % 4

    def slot_at(y, z):
        return ((y + SIDE) % SIDE) * SIDE + (z + SIDE) % SIDE

    barrier = pltpu.get_barrier_semaphore()

    def greet(i, _):
        pl.semaphore_signal(barrier, inc=1, device_id={"slot": (me + i) % n_slot}, device_id_type=MESH)
        return 0

    lax.fori_loop(1, n_slot, greet, 0)
    pl.semaphore_signal(barrier, inc=1, device_id={"conv": sibling}, device_id_type=MESH)
    pl.semaphore_signal(barrier, inc=1, device_id={"conv": partner}, device_id_type=MESH)

    loads = []
    for i, (source, target) in enumerate(((query_in, q_all), (grad_in, g_all))):
        for k in range(kv_count):
            loads.append(pltpu.make_async_copy(source.at[:, k * group : (k + 1) * group, :], target.at[k, me], load_sem.at[i, k]))
    moments = [pltpu.make_async_copy(x, y, load_sem.at[2, 1 + i]) for i, (x, y) in enumerate(((first_in, first_out), (second_in, second_out)))]
    cache_load = pltpu.make_async_copy(cache_in, stage, load_sem.at[2, 0])
    for load in loads:
        load.start()
    cache_load.start()
    small = [pltpu.make_async_copy(x, y, load_sem.at[i, 2]) for i, (x, y) in enumerate(((position_hbm, position_in), (offset_hbm, offset_in)))]
    for load in small:
        load.start()
    for load in loads:
        load.wait()

    pl.semaphore_wait(barrier, n_slot + 1)

    def gather_copy(tensor, k, block, device):
        view = (q_all, g_all)[tensor].at[k, block]
        return pltpu.make_async_remote_copy(
            src_ref=view,
            dst_ref=view,
            send_sem=gather_send.at[tensor, k],
            recv_sem=gather_recv.at[tensor, k, block],
            device_id={"slot": device},
            device_id_type=MESH,
        )

    def ring(tensor, first, step):
        along_y = (tensor == 0) == first
        return slot_at(my_y + step, my_z) if along_y else slot_at(my_y, my_z + step)

    def gather_own(k):
        for first in (True, False):
            for tensor in (0, 1):
                for step in (1, -1, 2):
                    gather_copy(tensor, k, me, ring(tensor, first, step)).start()

    def gather_turn(k):
        for step in (1, -1, 2):
            for tensor in (0, 1):
                gather_copy(tensor, k, ring(tensor, True, step), me).wait_recv()

    def gather_relay(k):
        for step in (1, -1, 2):
            for tensor in (0, 1):
                block = ring(tensor, True, step)
                for onward in (1, -1, 2):
                    gather_copy(tensor, k, block, ring(tensor, False, onward)).start()

    def gather_wait(k, dy, dz):
        for tensor, last in ((0, dz), (1, dy)):
            if last != 0:
                gather_copy(tensor, k, slot_at(my_y + dy, my_z + dz), me).wait_recv()

    gather_own(0)
    for load in moments:
        load.start()
    for load in small + [cache_load]:
        load.wait()
    for k in range(kv_count):
        key = stage[0, pl.ds(k, slots, stride=kv_count), :]
        key_ref[k] = key.astype(BF16)
        key_t_ref[k] = key.T.astype(BF16)
        value_ref[k] = stage[1, pl.ds(k, slots, stride=kv_count), :].astype(BF16)
    key_grad[...] = jnp.zeros_like(key_grad)
    value_grad[...] = jnp.zeros_like(value_grad)
    for i in range(slots // 128):
        row = offset_in[i : i + 1].astype(F32)
        offset_ref[i * 128 : (i + 1) * 128] = jnp.broadcast_to(row, (128, 128)).T
    spread = lax.broadcasted_iota(jnp.int32, (own_rows, width), 1) // group == lax.broadcasted_iota(jnp.int32, (own_rows, width), 0)
    for i in range(n_slot * own_rows // 128):
        rows = jnp.broadcast_to(position_in[i : i + 1].astype(F32), (128, 128)).T
        for j in range(128 // own_rows):
            mine = lanes(rows[j * own_rows : (j + 1) * own_rows], width)
            position_ref[i * (128 // own_rows) + j] = jnp.where(spread, mine, 0.0).sum(0, keepdims=True)

    def all_slots(k, source, target, send_sem, recv_sem, own_source):
        def send(i, _):
            other = (me + i) % n_slot
            pltpu.make_async_remote_copy(
                src_ref=source.at[k, me if own_source else other],
                dst_ref=target.at[k, me],
                send_sem=send_sem.at[k],
                recv_sem=recv_sem.at[k],
                device_id={"slot": other},
                device_id_type=MESH,
            ).start()
            return 0

        lax.fori_loop(1, n_slot, send, 0)

    def wait_all(k, ref, sem):
        view = ref.at[k, pl.ds(0, n_slot - 1)]
        pltpu.make_async_copy(view, view, sem.at[k]).wait()

    def stats_out(k):
        all_slots(k, own_stats, stats_in, stats_send, stats_recv, False)

    def stats_combine(k):
        wait_all(k, stats_in, stats_recv)
        stats_in[k, me] = own_stats[k, me]
        every = stats_in[k]
        top = every[:, 0:2].max(0)
        fade = jnp.exp2(every[:, 0:2] - top[None])
        total = (every[:, 2:4] * fade).sum(0)
        row_sum = (every[:, 4:6] * fade).sum(0) / total
        known[k, me, 0:2] = top + jnp.log2(total)
        known[k, me, 2:4] = row_sum
        all_slots(k, known, known, known_send, known_recv, True)

    def reduce_copy(color, k, source, target, recv_sem, device):
        return pltpu.make_async_remote_copy(
            src_ref=source,
            dst_ref=target,
            send_sem=reduce_send.at[k, color],
            recv_sem=recv_sem,
            device_id={"slot": device},
            device_id_type=MESH,
        )

    quarter = head_width // 4

    def reduce_event(k, color, da, db):
        dy, dz = (da, db) if color == 0 else (db, da)
        block = slot_at(my_y + dy, my_z + dz)
        a_at = ((my_y if color == 0 else my_z) + da) % SIDE
        mine = terms.at[k, color, block]

        def arrived(target, sem):
            pltpu.make_async_copy(target, target, sem).wait()
            return target[...].astype(F32)

        def add(side, target, sem):
            rows = pl.ds(side * quarter, quarter)
            mine[rows] = (mine[rows].astype(F32) + arrived(target, sem)).astype(BF16)

        def pieces(target, sems, first, index):
            for side, step in ((0, 1), (1, -1)):
                place = (k, color, side) + index
                rows = mine.at[pl.ds(side * quarter, quarter)]
                reduce_copy(color, k, rows, target.at[place], sems.at[place], ring(color, first, step)).start()

        def onward(target, sems, first, index, side):
            place = (k, color, side) + index
            reduce_copy(color, k, mine, target.at[place], sems.at[place], ring(color, first, 1 - 2 * side)).start()

        if db == 2:
            pieces(far_one, far_one_recv, False, (a_at,))
        elif db != 0:
            side = db // 2
            place = (k, color, side, a_at)
            add(side, far_one.at[place], far_one_recv.at[place])
            onward(near_one, near_one_recv, False, (a_at,), side)
        else:
            total = mine[...].astype(F32)
            for side in (0, 1):
                place = (k, color, side, a_at)
                total = total + arrived(near_one.at[place], near_one_recv.at[place])
            mine[...] = total.astype(BF16)
            if da == 2:
                pieces(far_two, far_two_recv, True, ())
            elif da != 0:
                side = da // 2
                place = (k, color, side)
                add(side, far_two.at[place], far_two_recv.at[place])
                onward(near_two, near_two_recv, True, (), side)

    def reduce_stage(k, stage):
        for event in REDUCE[stage]:
            reduce_event(k, *event)

    def reduce_end(k):
        sums = []
        for color in (0, 1):
            total = terms[k, color, me].astype(F32)
            for side in (0, 1):
                place = (k, color, side)
                view = near_two.at[place]
                pltpu.make_async_copy(view, view, near_two_recv.at[place]).wait()
                total = total + view[...].astype(F32)
            sums.append(total)
        rows = jnp.concatenate(sums, axis=0).T.reshape(own_rows, group, head_width)
        query_grad_out[:, k * group : (k + 1) * group, :] = rows

    half = slots // 2

    def conv_copy(hop, k, i, device):
        source, target = ((core_out, core_in), (chip_out, chip_in), (total_out, total_in))[hop]
        return pltpu.make_async_remote_copy(
            src_ref=source.at[k, i],
            dst_ref=target.at[k, i],
            send_sem=conv_send.at[k, hop, i],
            recv_sem=conv_recv.at[k, hop, i],
            device_id={"conv": device},
            device_id_type=MESH,
        )

    def own_grad(k, i, owner):
        rows = pl.ds(pl.multiple_of(owner * half, half), half)
        return key_grad[k, rows, :] * scale if i == 0 else value_grad[k, rows, :]

    def store_total(k, i, owner, value):
        place = pl.ds(pl.multiple_of(owner * (half * kv_count), half * kv_count) + k, half, stride=kv_count)
        slot_grad_out[i, place, :] = value

    def conv_one(k):
        for i in (0, 1):
            core_out[k, i] = own_grad(k, i, 1 - core).astype(BF16)
            conv_copy(0, k, i, sibling).start()

    def conv_two(k):
        for i in (0, 1):
            conv_copy(0, k, i, sibling).wait_recv()
            chip_out[k, i] = (own_grad(k, i, core) + core_in[k, i].astype(F32)).astype(BF16)
            conv_copy(1, k, i, partner).start()

    def conv_three(k):
        for i in (0, 1):
            conv_copy(1, k, i, partner).wait_recv()
            total_out[k, i] = (chip_out[k, i].astype(F32) + chip_in[k, i].astype(F32)).astype(BF16)
            conv_copy(2, k, i, sibling).start()
            store_total(k, i, core, total_out[k, i].astype(F32))

    def conv_end(k):
        for i in (0, 1):
            conv_copy(2, k, i, sibling).wait_recv()
            store_total(k, i, 1 - core, total_in[k, i].astype(F32))
            for hop in range(3):
                conv_copy(hop, k, i, sibling).wait_send()

    def step(t, _):
        def at_step(at):
            return pl.when(t == at)

        for work, k, at in (
            (gather_turn, 0, 0),
            (gather_relay, 0, 0),
            (gather_own, 1, 0),
            (stats_out, 0, 8),
            (gather_turn, 1, 8),
            (stats_combine, 0, 11),
            (gather_relay, 1, 11),
            (stats_out, 1, 20),
            (stats_combine, 1, 22),
        ):

            @at_step(at)
            def _():
                work(k)

        for k, at in ((0, 11), (1, 24)):

            @at_step(at)
            def _():
                wait_all(k, known, known_recv)

        for at, (which, k, pair) in enumerate(STEPS):
            if which == 0:

                @at_step(at)
                def _():
                    for place in NEAR_FIRST[2 * pair : 2 * pair + 2]:
                        gather_wait(k, *place)

        for stage, at in enumerate(REDUCE_AT[0]):
            also = REDUCE_AT[1][stage] if stage < len(REDUCE_AT[1]) else at

            @pl.when((t == at) | (t == also))
            def _():
                reduce_stage(jnp.where(t == at, 0, 1), stage)

        for work, at in ((conv_one, 24), (conv_two, 26), (conv_three, 30)):

            @at_step(at)
            def _():
                work(0)

        which, k, pair = (looked_up([entry[i] for entry in STEPS], t) for i in range(3))

        def blocks_of(order):
            found = []
            for i in (0, 1):
                dy, dz = (looked_up([d[axis] for d in order[i::2]], pair) for axis in (0, 1))
                found.append(slot_at(my_y + dy, my_z + dz))
            return found

        def rows_of(ref, blocks):
            return jnp.concatenate([ref[k, block].reshape(width, head_width) for block in blocks], axis=0)

        def positions_of(blocks):
            return jnp.concatenate([position_ref[block] for block in blocks], axis=1)

        @pl.when(which == 0)
        def _():
            blocks = blocks_of(NEAR_FIRST)
            stats = stats_pass(
                rows_of(q_all, blocks),
                rows_of(g_all, blocks),
                key_ref.at[k],
                value_ref.at[k],
                offset_ref,
                positions_of(blocks),
                scale2,
                STATS_CHUNK,
            )
            for i, stat in enumerate(stats):
                for j in range(2 * width // 128):
                    row = i * (width // 128) + j % (width // 128)
                    own_stats[k, blocks[j * 128 // width], row : row + 1] = stat[:, j * 128 : (j + 1) * 128]

        @pl.when(which == 1)
        def _():
            blocks = blocks_of(FAR_FIRST)
            stats = [known[k, block] for block in blocks]
            both = [jnp.concatenate([stat[row : row + 1] for stat in stats for row in (i, i + 1)], axis=1) for i in (0, 2)]
            found = grad_pass(
                rows_of(q_all, blocks),
                rows_of(g_all, blocks),
                key_ref.at[k],
                value_ref.at[k],
                key_t_ref.at[k],
                offset_ref,
                positions_of(blocks),
                both[0],
                both[1],
                key_grad.at[k],
                value_grad.at[k],
                scale2,
                GRADS_CHUNK,
            )
            found = (found * scale).astype(BF16)
            for i, block in enumerate(blocks):
                for color in (0, 1):
                    terms[k, color, block] = found[color * head_width // 2 : (color + 1) * head_width // 2, i * width : (i + 1) * width]

        return 0

    lax.fori_loop(0, len(STEPS), step, 0)
    conv_one(1)
    reduce_stage(1, 7)
    conv_two(1)
    reduce_end(0)
    conv_end(0)
    reduce_stage(1, 8)
    reduce_stage(1, 9)
    conv_three(1)
    reduce_end(1)
    for k in range(kv_count):
        for tensor, buffer in enumerate((q_all, g_all)):
            view = buffer.at[k, pl.ds(0, n_slot - 1)]
            pltpu.make_async_copy(view, view, gather_send.at[tensor, k]).wait()
        wait_all(k, own_stats, stats_send)
        wait_all(k, known, known_send)
        for color in (0, 1):
            view = terms.at[k, color, pl.ds(0, n_slot - 1)]
            pltpu.make_async_copy(view, view, reduce_send.at[k, color]).wait()
    for load in moments:
        load.wait()
    conv_end(1)


def local(queries, out_grad, row_positions, slot_offsets, cache, first_moment, second_moment):
    own_rows, head_count, head_width = queries.shape
    kv_count, slots = cache.shape[2], cache.shape[1]
    group = head_count // kv_count
    blocks = row_positions.shape[0] // own_rows
    width = own_rows * group
    scale = 1.0 / math.sqrt(head_width)

    flat = (2, slots * kv_count, head_width)

    vmem = pl.BlockSpec(memory_space=pltpu.VMEM)
    hbm = pl.BlockSpec(memory_space=pltpu.HBM)
    dma = pltpu.SemaphoreType.DMA
    rows_all = pltpu.VMEM((kv_count, blocks, own_rows, group, head_width), BF16)
    in_hbm = lambda x: pltpu.with_memory_space_constraint(x, pltpu.HBM)
    slots_half = pltpu.VMEM((kv_count, slots, head_width), BF16)
    slots_full = pltpu.VMEM((kv_count, slots, head_width), F32)
    stats = pltpu.VMEM((kv_count, blocks, 8, 128), F32)
    conv_half = pltpu.VMEM((kv_count, 2, slots // 2, head_width), BF16)
    slot_grad, query_grad, cache_flat, first_flat, second_flat = pl.pallas_call(
        functools.partial(whole_kernel, scale),
        out_shape=(jax.ShapeDtypeStruct(flat, F32), jax.ShapeDtypeStruct(queries.shape, F32)) + (jax.ShapeDtypeStruct(flat, F32),) * 3,
        in_specs=[hbm] * 7,
        out_specs=(vmem,) * 5,
        scratch_shapes=[
            pltpu.VMEM((blocks * own_rows // 128, 128), jnp.int32),
            pltpu.VMEM((slots // 128, 128), jnp.int32),
            pltpu.VMEM((blocks, 1, width), F32),
            pltpu.VMEM((slots, 128), F32),
            rows_all,
            rows_all,
            slots_half,
            slots_half,
            pltpu.VMEM((kv_count, head_width, slots), BF16),
            slots_full,
            slots_full,
            stats,
            stats,
            stats,
            pltpu.VMEM((kv_count, 2, blocks, head_width // 2, width), BF16),
            pltpu.VMEM((kv_count, 2, 2, SIDE, head_width // 4, width), BF16),
            pltpu.VMEM((kv_count, 2, 2, SIDE, head_width // 2, width), BF16),
            pltpu.VMEM((kv_count, 2, 2, head_width // 4, width), BF16),
            pltpu.VMEM((kv_count, 2, 2, head_width // 2, width), BF16),
        ]
        + [conv_half] * 6
        + [
            dma((3, 4)),
            dma((2, kv_count)),
            dma((2, kv_count, blocks)),
            dma((kv_count,)),
            dma((kv_count,)),
            dma((kv_count,)),
            dma((kv_count,)),
            dma((kv_count, 2)),
            dma((kv_count, 2, 2, SIDE)),
            dma((kv_count, 2, 2, SIDE)),
            dma((kv_count, 2, 2)),
            dma((kv_count, 2, 2)),
            dma((kv_count, 3, 2)),
            dma((kv_count, 3, 2)),
        ],
        compiler_params=pltpu.CompilerParams(collective_id=0, has_side_effects=True, vmem_limit_bytes=34 << 20),
        name="whole",
    )(in_hbm(queries), in_hbm(out_grad), in_hbm(row_positions.reshape(-1, 128)), in_hbm(slot_offsets.reshape(-1, 128)), *(in_hbm(x.reshape(flat)) for x in (cache, first_moment, second_moment)))

    new_first = beta_one * first_flat + (1.0 - beta_one) * slot_grad
    new_second = beta_two * second_flat + (1.0 - beta_two) * slot_grad * slot_grad
    first_fix = 1.0 - beta_one**STEP
    second_fix = 1.0 - beta_two**STEP
    new_cache = cache_flat - learn_rate * (new_first / first_fix) / (jnp.sqrt(new_second / second_fix) + adam_eps)
    return tuple(x.reshape(cache.shape) for x in (new_cache, new_first, new_second)) + (query_grad,)


def solution(mesh):
    rows = P(("conv", "slot"), "head", None)
    slots = P(None, "slot", "head", None)
    return jax.shard_map(
        local,
        mesh=mesh,
        in_specs=(rows, rows, P("conv"), P("slot"), slots, slots, slots),
        out_specs=(slots, slots, slots, rows),
        check_vma=False,
    )
```

time: 121 us -> 95.8 us (0.79)
  Pallas kernels: 108 us -> 90.8 us
  local copies, waits for them, and re-layouts: 6.44 us -> 0.7 us
  other arithmetic: 5.46 us -> 3.47 us
    pallas_call x1, Pallas kernels: 108 us -> 90.8 us  [local(): pl.pallas_call(functools.partial(whole_kernel, scale), out_shape=(jax.Sha...]
    unnamed x11 -> x1, local copies, waits for them, and re-layouts: 4.6 us -> 0.7 us
    mul x2 -> x0, other arithmetic: 2.16 us -> none  [the longest x1 1.08 us: local(): new_first = beta_one * first_flat + (1.0 - beta_one) * slot_grad]
    broadcast_in_dim x4 -> x0, local copies, waits for them, and re-layouts: 1.84 us -> none  [the longest x3 0.96 us: local(): positions = jnp.repeat(row_positions, group).reshape(blocks, 1, width)]
where the time goes in v2:
time: 95.8 us; the launch traced here: 95.6 us
  Pallas kernels  90.8 us (95%)
  other arithmetic  3.47 us (4%)
    pallas_call x1, Pallas kernels, local(): pl.pallas_call(functools.partial(whole_kernel, scale), out_shape=(jax.Sha...  90.8 us
    sub x1, other arithmetic, local(): cache_flat - learn_rate * (new_first / first_fix) / (jnp.sqrt(new_second...  3.47 us

profile of v2, /device:TPU:1, one launch (start us, length us, event | category | flops | bytes accessed | tf_op | source)
XLA Modules:
  0.0 95.6 jit_solution(11962394347367453379)
XLA Ops:
  0.6 90.8 %whole.1 = (f32[2,2048,128]{2,1,0:T(8,128)S(1)}, f32[16,32,128]{2,1,0:T(8,128)S(1)}, f32[2,2048,128]{2,1,0:T(8,128)S(1)}, f32[2,2048,128]{2,1,0:T(8,128)S(1)}, f32[2,2048,128]{2,1,0:T(8,128)S(1)}) custom-call(bf16[16,32,128]{2,1,0:T(8,128)(2,1)} %query_in.1, bf16[16,32,128]{2,1,0:T(8,128)(2,1)} %grad_in.1, s32[2,128]{1,0:T(2,128)} %bitcast.15, ...), custom_call_target="tpu_custom_call" | custom-call | tf_op jit(solution)/shard_map/whole/pallas_call | solution.py:571
  91.5 3.5 %divide_subtract_fusion = (f32[2,2048,128]{2,1,0:T(8,128)}, f32[2,2048,128]{2,1,0:T(8,128)}, f32[2,2048,128]{2,1,0:T(8,128)}) fusion(f32[2,2048,128]{2,1,0:T(8,128)S(1)} %get-tuple-element.9, f32[2,2048,128]{2,1,0:T(8,128)S(1)} %get-tuple-element.11, f32[2,2048,128]{2,1,0:T(8,128)S(1)} %get-tuple-element.10, f32[2,2048,128]{2,1,0:T(8,128)S(1)} %get-tuple-element.12), kind=kLoop, calls=%fused_computation.2 | loop fusion | flops 6291456 | bytes 14680064 | tf_op jit(solution)/shard_map/sub | solution.py:622
  94.9 0.7 copy.12

commit v3 on v2

--- a/solution.py
+++ b/solution.py
@@ -79,25 +79,11 @@
 STEPS = (
     [(0, 0, p) for p in range(8)]
     + [(0, 1, p) for p in range(3)]
-    + [(1, 0, p) for p in range(4)]
+    + [(1, 0, p) for p in range(2)]
     + [(0, 1, p) for p in range(3, 8)]
-    + [(1, 0, p) for p in range(4, 8)]
+    + [(1, 0, p) for p in range(2, 8)]
     + [(1, 1, p) for p in range(8)]
 )
-REDUCE = (
-    ((0, 2, 2), (1, 2, 2), (1, 1, 2)),
-    ((0, 1, 2), (1, 3, 2)),
-    ((0, 3, 2), (0, 2, 1), (0, 2, 3), (1, 0, 2), (1, 2, 1), (1, 2, 3)),
-    ((0, 0, 2), (0, 1, 1), (1, 1, 1)),
-    ((0, 1, 3), (0, 3, 1), (0, 2, 0), (1, 1, 3), (1, 3, 1), (1, 2, 0)),
-    ((0, 3, 3), (1, 3, 3), (1, 0, 1)),
-    ((0, 0, 1), (0, 1, 0), (1, 0, 3), (1, 1, 0)),
-    ((0, 0, 3), (0, 3, 0), (1, 3, 0)),
-    (),
-    ((0, 0, 0), (1, 0, 0)),
-)
-REDUCE_AT = ((13, 14, 15, 17, 21, 22, 23, 24, 25, 26), (25, 26, 27, 28, 29, 30, 31))
-
 
 def looked_up(table, at):
     found = jnp.int32(table[0])
@@ -136,10 +122,7 @@
     stats_in,
     known,
     terms,
-    far_one,
-    near_one,
-    far_two,
-    near_two,
+    terms_in,
     core_out,
     core_in,
     chip_out,
@@ -153,11 +136,8 @@
     stats_recv,
     known_send,
     known_recv,
-    reduce_send,
-    far_one_recv,
-    near_one_recv,
-    far_two_recv,
-    near_two_recv,
+    terms_send,
+    terms_recv,
     conv_send,
     conv_recv,
 ):
@@ -225,14 +205,16 @@
                 for step in (1, -1, 2):
                     gather_copy(tensor, k, me, ring(tensor, first, step)).start()
 
-    def gather_turn(k):
+    def gather_turn(k, relay=False):
         for step in (1, -1, 2):
             for tensor in (0, 1):
                 gather_copy(tensor, k, ring(tensor, True, step), me).wait_recv()
-
-    def gather_relay(k):
-        for step in (1, -1, 2):
-            for tensor in (0, 1):
+                if relay:
+                    gather_relay(k, (tensor,), (step,))
+
+    def gather_relay(k, tensors=(0, 1), steps=(1, -1, 2)):
+        for step in steps:
+            for tensor in tensors:
                 block = ring(tensor, True, step)
                 for onward in (1, -1, 2):
                     gather_copy(tensor, k, block, ring(tensor, False, onward)).start()
@@ -298,79 +280,29 @@
         known[k, me, 2:4] = row_sum
         all_slots(k, known, known, known_send, known_recv, True)
 
-    def reduce_copy(color, k, source, target, recv_sem, device):
+    def terms_copy(k, block):
         return pltpu.make_async_remote_copy(
-            src_ref=source,
-            dst_ref=target,
-            send_sem=reduce_send.at[k, color],
-            recv_sem=recv_sem,
-            device_id={"slot": device},
+            src_ref=terms.at[k, block],
+            dst_ref=terms_in.at[k, me],
+            send_sem=terms_send.at[k],
+            recv_sem=terms_recv.at[k],
+            device_id={"slot": block},
             device_id_type=MESH,
         )
 
-    quarter = head_width // 4
-
-    def reduce_event(k, color, da, db):
-        dy, dz = (da, db) if color == 0 else (db, da)
-        block = slot_at(my_y + dy, my_z + dz)
-        a_at = ((my_y if color == 0 else my_z) + da) % SIDE
-        mine = terms.at[k, color, block]
-
-        def arrived(target, sem):
-            pltpu.make_async_copy(target, target, sem).wait()
-            return target[...].astype(F32)
-
-        def add(side, target, sem):
-            rows = pl.ds(side * quarter, quarter)
-            mine[rows] = (mine[rows].astype(F32) + arrived(target, sem)).astype(BF16)
-
-        def pieces(target, sems, first, index):
-            for side, step in ((0, 1), (1, -1)):
-                place = (k, color, side) + index
-                rows = mine.at[pl.ds(side * quarter, quarter)]
-                reduce_copy(color, k, rows, target.at[place], sems.at[place], ring(color, first, step)).start()
-
-        def onward(target, sems, first, index, side):
-            place = (k, color, side) + index
-            reduce_copy(color, k, mine, target.at[place], sems.at[place], ring(color, first, 1 - 2 * side)).start()
-
-        if db == 2:
-            pieces(far_one, far_one_recv, False, (a_at,))
-        elif db != 0:
-            side = db // 2
-            place = (k, color, side, a_at)
-            add(side, far_one.at[place], far_one_recv.at[place])
-            onward(near_one, near_one_recv, False, (a_at,), side)
-        else:
-            total = mine[...].astype(F32)
-            for side in (0, 1):
-                place = (k, color, side, a_at)
-                total = total + arrived(near_one.at[place], near_one_recv.at[place])
-            mine[...] = total.astype(BF16)
-            if da == 2:
-                pieces(far_two, far_two_recv, True, ())
-            elif da != 0:
-                side = da // 2
-                place = (k, color, side)
-                add(side, far_two.at[place], far_two_recv.at[place])
-                onward(near_two, near_two_recv, True, (), side)
-
-    def reduce_stage(k, stage):
-        for event in REDUCE[stage]:
-            reduce_event(k, *event)
-
-    def reduce_end(k):
-        sums = []
-        for color in (0, 1):
-            total = terms[k, color, me].astype(F32)
-            for side in (0, 1):
-                place = (k, color, side)
-                view = near_two.at[place]
-                pltpu.make_async_copy(view, view, near_two_recv.at[place]).wait()
-                total = total + view[...].astype(F32)
-            sums.append(total)
-        rows = jnp.concatenate(sums, axis=0).T.reshape(own_rows, group, head_width)
-        query_grad_out[:, k * group : (k + 1) * group, :] = rows
+    def terms_out(k, pair):
+        for dy, dz in FAR_FIRST[2 * pair : 2 * pair + 2]:
+            if (dy, dz) != (0, 0):
+                terms_copy(k, slot_at(my_y + dy, my_z + dz)).start()
+
+    def terms_end(k):
+        wait_all(k, terms_in, terms_recv)
+
+        def add(i, total):
+            return total + terms_in[k, (me + i) % n_slot].astype(F32)
+
+        total = lax.fori_loop(1, n_slot, add, terms[k, me].astype(F32))
+        query_grad_out[:, k * group : (k + 1) * group, :] = total.T.reshape(own_rows, group, head_width)
 
     half = slots // 2
 
@@ -423,15 +355,14 @@
             return pl.when(t == at)
 
         for work, k, at in (
-            (gather_turn, 0, 0),
-            (gather_relay, 0, 0),
+            (functools.partial(gather_turn, relay=True), 0, 0),
             (gather_own, 1, 0),
             (stats_out, 0, 8),
             (gather_turn, 1, 8),
             (stats_combine, 0, 11),
             (gather_relay, 1, 11),
-            (stats_out, 1, 20),
-            (stats_combine, 1, 22),
+            (stats_out, 1, 18),
+            (stats_combine, 1, 21),
         ):
 
             @at_step(at)
@@ -452,14 +383,14 @@
                     for place in NEAR_FIRST[2 * pair : 2 * pair + 2]:
                         gather_wait(k, *place)
 
-        for stage, at in enumerate(REDUCE_AT[0]):
-            also = REDUCE_AT[1][stage] if stage < len(REDUCE_AT[1]) else at
-
-            @pl.when((t == at) | (t == also))
-            def _():
-                reduce_stage(jnp.where(t == at, 0, 1), stage)
-
-        for work, at in ((conv_one, 24), (conv_two, 26), (conv_three, 30)):
+        for at, (which, k, pair) in enumerate(STEPS[:-1]):
+            if which == 1:
+
+                @at_step(at + 1)
+                def _():
+                    terms_out(k, pair)
+
+        for work, at in ((conv_one, 24), (conv_two, 26)):
 
             @at_step(at)
             def _():
@@ -520,30 +451,26 @@
             )
             found = (found * scale).astype(BF16)
             for i, block in enumerate(blocks):
-                for color in (0, 1):
-                    terms[k, color, block] = found[color * head_width // 2 : (color + 1) * head_width // 2, i * width : (i + 1) * width]
+                terms[k, block] = found[:, i * width : (i + 1) * width]
 
         return 0
 
     lax.fori_loop(0, len(STEPS), step, 0)
+    terms_out(*STEPS[-1][1:])
     conv_one(1)
-    reduce_stage(1, 7)
+    conv_three(0)
     conv_two(1)
-    reduce_end(0)
+    terms_end(0)
     conv_end(0)
-    reduce_stage(1, 8)
-    reduce_stage(1, 9)
+    terms_end(1)
     conv_three(1)
-    reduce_end(1)
     for k in range(kv_count):
         for tensor, buffer in enumerate((q_all, g_all)):
             view = buffer.at[k, pl.ds(0, n_slot - 1)]
             pltpu.make_async_copy(view, view, gather_send.at[tensor, k]).wait()
         wait_all(k, own_stats, stats_send)
         wait_all(k, known, known_send)
-        for color in (0, 1):
-            view = terms.at[k, color, pl.ds(0, n_slot - 1)]
-            pltpu.make_async_copy(view, view, reduce_send.at[k, color]).wait()
+        wait_all(k, terms, terms_send)
     for load in moments:
         load.wait()
     conv_end(1)
@@ -588,11 +515,8 @@
             stats,
             stats,
             stats,
-            pltpu.VMEM((kv_count, 2, blocks, head_width // 2, width), BF16),
-            pltpu.VMEM((kv_count, 2, 2, SIDE, head_width // 4, width), BF16),
-            pltpu.VMEM((kv_count, 2, 2, SIDE, head_width // 2, width), BF16),
-            pltpu.VMEM((kv_count, 2, 2, head_width // 4, width), BF16),
-            pltpu.VMEM((kv_count, 2, 2, head_width // 2, width), BF16),
+            pltpu.VMEM((kv_count, blocks, head_width, width), BF16),
+            pltpu.VMEM((kv_count, blocks, head_width, width), BF16),
         ]
         + [conv_half] * 6
         + [
@@ -603,15 +527,12 @@
             dma((kv_count,)),
             dma((kv_count,)),
             dma((kv_count,)),
-            dma((kv_count, 2)),
-            dma((kv_count, 2, 2, SIDE)),
-            dma((kv_count, 2, 2, SIDE)),
-            dma((kv_count, 2, 2)),
-            dma((kv_count, 2, 2)),
+            dma((kv_count,)),
+            dma((kv_count,)),
             dma((kv_count, 3, 2)),
             dma((kv_count, 3, 2)),
         ],
-        compiler_params=pltpu.CompilerParams(collective_id=0, has_side_effects=True, vmem_limit_bytes=34 << 20),
+        compiler_params=pltpu.CompilerParams(collective_id=0, has_side_effects=True, vmem_limit_bytes=36 << 20),
         name="whole",
     )(in_hbm(queries), in_hbm(out_grad), in_hbm(row_positions.reshape(-1, 128)), in_hbm(slot_offsets.reshape(-1, 128)), *(in_hbm(x.reshape(flat)) for x in (cache, first_moment, second_moment)))
 

time: 95.8 us -> 95.2 us (level)
  no operation moved by 1% of the time
where the time goes in v3:
time: 95.2 us; the launch traced here: 95 us
  Pallas kernels  90.2 us (95%)
  other arithmetic  3.47 us (4%)
    pallas_call x1, Pallas kernels, local(): pl.pallas_call(functools.partial(whole_kernel, scale), out_shape=(jax.Sha...  90.2 us
    sub x1, other arithmetic, local(): cache_flat - learn_rate * (new_first / first_fix) / (jnp.sqrt(new_second...  3.47 us

profile of v3, /device:TPU:1, one launch (start us, length us, event | category | flops | bytes accessed | tf_op | source)
XLA Modules:
  0.0 95.0 jit_solution(10603697117451070936)
XLA Ops:
  0.6 90.2 %whole.1 = (f32[2,2048,128]{2,1,0:T(8,128)S(1)}, f32[16,32,128]{2,1,0:T(8,128)S(1)}, f32[2,2048,128]{2,1,0:T(8,128)S(1)}, f32[2,2048,128]{2,1,0:T(8,128)S(1)}, f32[2,2048,128]{2,1,0:T(8,128)S(1)}) custom-call(bf16[16,32,128]{2,1,0:T(8,128)(2,1)} %query_in.1, bf16[16,32,128]{2,1,0:T(8,128)(2,1)} %grad_in.1, s32[2,128]{1,0:T(2,128)} %bitcast.15, ...), custom_call_target="tpu_custom_call" | custom-call | tf_op jit(solution)/shard_map/whole/pallas_call | solution.py:498
  90.9 3.5 %divide_subtract_fusion = (f32[2,2048,128]{2,1,0:T(8,128)}, f32[2,2048,128]{2,1,0:T(8,128)}, f32[2,2048,128]{2,1,0:T(8,128)}) fusion(f32[2,2048,128]{2,1,0:T(8,128)S(1)} %get-tuple-element.9, f32[2,2048,128]{2,1,0:T(8,128)S(1)} %get-tuple-element.11, f32[2,2048,128]{2,1,0:T(8,128)S(1)} %get-tuple-element.10, f32[2,2048,128]{2,1,0:T(8,128)S(1)} %get-tuple-element.12), kind=kLoop, calls=%fused_computation.2 | loop fusion | flops 6291456 | bytes 14680064 | tf_op jit(solution)/shard_map/sub | solution.py:543
  94.3 0.7 copy.12

commit v4 on v2

--- a/solution.py
+++ b/solution.py
@@ -79,9 +79,9 @@
 STEPS = (
     [(0, 0, p) for p in range(8)]
     + [(0, 1, p) for p in range(3)]
-    + [(1, 0, p) for p in range(4)]
+    + [(1, 0, p) for p in range(2)]
     + [(0, 1, p) for p in range(3, 8)]
-    + [(1, 0, p) for p in range(4, 8)]
+    + [(1, 0, p) for p in range(2, 8)]
     + [(1, 1, p) for p in range(8)]
 )
 REDUCE = (
@@ -96,7 +96,7 @@
     (),
     ((0, 0, 0), (1, 0, 0)),
 )
-REDUCE_AT = ((13, 14, 15, 17, 21, 22, 23, 24, 25, 26), (25, 26, 27, 28, 29, 30, 31))
+REDUCE_AT = ((13, 15, 19, 20, 21, 22, 23, 24, 25, 26), (25, 26, 27, 28, 29, 30, 31))
 
 
 def looked_up(table, at):
@@ -225,14 +225,16 @@
                 for step in (1, -1, 2):
                     gather_copy(tensor, k, me, ring(tensor, first, step)).start()
 
-    def gather_turn(k):
+    def gather_turn(k, relay=False):
         for step in (1, -1, 2):
             for tensor in (0, 1):
                 gather_copy(tensor, k, ring(tensor, True, step), me).wait_recv()
-
-    def gather_relay(k):
-        for step in (1, -1, 2):
-            for tensor in (0, 1):
+                if relay:
+                    gather_relay(k, (tensor,), (step,))
+
+    def gather_relay(k, tensors=(0, 1), steps=(1, -1, 2)):
+        for step in steps:
+            for tensor in tensors:
                 block = ring(tensor, True, step)
                 for onward in (1, -1, 2):
                     gather_copy(tensor, k, block, ring(tensor, False, onward)).start()
@@ -423,15 +425,14 @@
             return pl.when(t == at)
 
         for work, k, at in (
-            (gather_turn, 0, 0),
-            (gather_relay, 0, 0),
+            (functools.partial(gather_turn, relay=True), 0, 0),
             (gather_own, 1, 0),
             (stats_out, 0, 8),
             (gather_turn, 1, 8),
             (stats_combine, 0, 11),
             (gather_relay, 1, 11),
-            (stats_out, 1, 20),
-            (stats_combine, 1, 22),
+            (stats_out, 1, 18),
+            (stats_combine, 1, 21),
         ):
 
             @at_step(at)
@@ -459,7 +460,7 @@
             def _():
                 reduce_stage(jnp.where(t == at, 0, 1), stage)
 
-        for work, at in ((conv_one, 24), (conv_two, 26), (conv_three, 30)):
+        for work, at in ((conv_one, 24), (conv_two, 26)):
 
             @at_step(at)
             def _():
@@ -527,8 +528,9 @@
 
     lax.fori_loop(0, len(STEPS), step, 0)
     conv_one(1)
+    conv_three(0)
+    conv_two(1)
     reduce_stage(1, 7)
-    conv_two(1)
     reduce_end(0)
     conv_end(0)
     reduce_stage(1, 8)

time: 95.8 us -> 94.7 us (0.989)
  Pallas kernels: 90.8 us -> 89.7 us
    pallas_call x1, Pallas kernels: 90.8 us -> 89.7 us  [local(): pl.pallas_call(functools.partial(whole_kernel, scale), out_shape=(jax.Sha...]
where the time goes in v4:
time: 94.7 us; the launch traced here: 94.5 us
  Pallas kernels  89.7 us (95%)
  other arithmetic  3.47 us (4%)
    pallas_call x1, Pallas kernels, local(): pl.pallas_call(functools.partial(whole_kernel, scale), out_shape=(jax.Sha...  89.7 us
    sub x1, other arithmetic, local(): cache_flat - learn_rate * (new_first / first_fix) / (jnp.sqrt(new_second...  3.47 us

profile of v4, /device:TPU:1, one launch (start us, length us, event | category | flops | bytes accessed | tf_op | source)
XLA Modules:
  0.0 94.5 jit_solution(17345567601339602679)
XLA Ops:
  0.6 89.7 %whole.1 = (f32[2,2048,128]{2,1,0:T(8,128)S(1)}, f32[16,32,128]{2,1,0:T(8,128)S(1)}, f32[2,2048,128]{2,1,0:T(8,128)S(1)}, f32[2,2048,128]{2,1,0:T(8,128)S(1)}, f32[2,2048,128]{2,1,0:T(8,128)S(1)}) custom-call(bf16[16,32,128]{2,1,0:T(8,128)(2,1)} %query_in.1, bf16[16,32,128]{2,1,0:T(8,128)(2,1)} %grad_in.1, s32[2,128]{1,0:T(2,128)} %bitcast.15, ...), custom_call_target="tpu_custom_call" | custom-call | tf_op jit(solution)/shard_map/whole/pallas_call | solution.py:573
  90.3 3.5 %divide_subtract_fusion = (f32[2,2048,128]{2,1,0:T(8,128)}, f32[2,2048,128]{2,1,0:T(8,128)}, f32[2,2048,128]{2,1,0:T(8,128)}) fusion(f32[2,2048,128]{2,1,0:T(8,128)S(1)} %get-tuple-element.9, f32[2,2048,128]{2,1,0:T(8,128)S(1)} %get-tuple-element.11, f32[2,2048,128]{2,1,0:T(8,128)S(1)} %get-tuple-element.10, f32[2,2048,128]{2,1,0:T(8,128)S(1)} %get-tuple-element.12), kind=kLoop, calls=%fused_computation.2 | loop fusion | flops 6291456 | bytes 14680064 | tf_op jit(solution)/shard_map/sub | solution.py:624
  93.8 0.7 copy.12
